TPU v7x, 32 devices: a whole 2x2x4 slice. The times are simulated.
32 devices in a mesh: rows: 8 (over z, y), heads: 4 (over x, core).
Axes of the slice: x: 2, y: 2, z: 4, core: 2. Of those that a mesh axis runs over, the one named last changes fastest.
Arguments:
- hidden_in: bfloat16 [64, 512, 768], P('rows', 'heads'), may hold values from -6 to 6
- lengths: int32 [64, 4], P('rows'), may hold values from 1 to 256, 512 in all within a row
- qkv_weight: bfloat16 [768, 2304], replicated, may hold values from -0.21875 to 0.21875
- query_bias: bfloat16 [768], replicated, may hold values from -3 to 3
- value_bias: bfloat16 [768], replicated, may hold values from -0.59765625 to 0.59765625
- out_weight: bfloat16 [768, 768], replicated, may hold values from -1.75 to 1.75
- out_bias: bfloat16 [768], replicated, may hold values from -1.1953125 to 1.1953125
- gain_one: bfloat16 [768], replicated, may hold values from 0.5 to 1.5
- shift_one: bfloat16 [768], replicated, may hold values from -1.1953125 to 1.1953125
- up_weight: bfloat16 [768, 3072], replicated, may hold values from -0.21875 to 0.21875
- up_bias: bfloat16 [3072], replicated, may hold values from -1.1953125 to 1.1953125
- down_weight: bfloat16 [3072, 768], replicated, may hold values from -0.15625 to 0.15625
- down_bias: bfloat16 [768], replicated, may hold values from -1.1953125 to 1.1953125
- gain_two: bfloat16 [768], replicated, may hold values from 0.5 to 1.5
- shift_two: bfloat16 [768], replicated, may hold values from -1.1953125 to 1.1953125
- cotangent: bfloat16 [64, 512, 768], P('rows', 'heads'), may hold values from -6 to 6
Outputs:
- layer_out: bfloat16 [64, 512, 768], P('rows', 'heads')
- input_grad: float32 [64, 512, 768], P('rows', 'heads')
- qkv_grad: float32 [768, 2304], P('rows', 'heads')
- querybias_grad: float32 [768], replicated
- valuebias_grad: float32 [768], replicated
- outweight_grad: float32 [768, 768], P('rows', 'heads')
- outbias_grad: float32 [768], replicated
- gainone_grad: float32 [768], replicated
- shiftone_grad: float32 [768], replicated
- upweight_grad: float32 [768, 3072], P('rows', 'heads')
- upbias_grad: float32 [3072], replicated
- downweight_grad: float32 [3072, 768], P('rows', 'heads')
- downbias_grad: float32 [768], replicated
- gaintwo_grad: float32 [768], replicated
- shifttwo_grad: float32 [768], replicated
Inputs may be any that keep to these rules, and one draw needn't show every extreme that they name: The 4 lengths of a packed row sum to 512; in every row the longest is 256.
All inputs are finite; a program needn't handle non-finite values.
Results may differ from a plain program's by a relative error of at most 0.017.
Values may be sent and summed in bfloat16 or wider, within the bound.
A program may use at most 192 MiB of HBM per device.

v0:
```python
import jax
import jax.numpy as jnp
from jax import lax
from jax.sharding import PartitionSpec as P

DH = 64
D = 768
L = 512


EPSILON = 1e-12
NEGATIVE = -1e30


def segment_ids(lengths):
    ends = jnp.cumsum(lengths, axis=-1)
    places = jnp.arange(L, dtype=jnp.int32)
    return jnp.sum((places[None, :, None] >= ends[:, None, :]).astype(jnp.int32), axis=-1)


def layer_norm(values, gain, shift):
    middle = jnp.mean(values, axis=-1, keepdims=True)
    center = values - middle
    spread = jnp.mean(center * center, axis=-1, keepdims=True)
    return center * lax.rsqrt(spread + EPSILON) * gain + shift


def exact_gelu(values):
    return jax.nn.gelu(values, approximate=False)


def masked_scores(query_heads, key_heads, query_seg, key_seg):
    scores = jnp.einsum(
        "qhd,khd->hqk", query_heads, key_heads, preferred_element_type=jnp.float32
    ) * DH ** (-0.5)
    same = query_seg[:, None] == key_seg[None, :]
    return jnp.where(same[None], scores, NEGATIVE)


def split_heads(values):
    return values.reshape(values.shape[0], values.shape[1] // DH, DH)


def attend_forward(queries, key_rows, value_rows, query_seg, key_seg):
    width = queries.shape[1]
    scores = masked_scores(split_heads(queries), split_heads(key_rows), query_seg, key_seg)
    peak = jnp.max(scores, axis=-1, keepdims=True)
    expos = jnp.exp(scores - peak)
    totals = jnp.sum(expos, axis=-1, keepdims=True)
    chance = (expos / totals).astype(jnp.bfloat16)
    context = jnp.einsum(
        "hqk,khd->qhd", chance, split_heads(value_rows), preferred_element_type=jnp.float32
    )
    return (
        context.reshape(queries.shape[0], width).astype(jnp.bfloat16),
        (peak + jnp.log(totals))[..., 0],
    )


def attend_backward(queries, key_rows, value_rows, context_grad, summary, query_seg, key_seg):
    width = queries.shape[1]
    query_heads = split_heads(queries)
    key_heads = split_heads(key_rows)
    value_heads = split_heads(value_rows)
    grad_heads = split_heads(context_grad)
    scores = masked_scores(query_heads, key_heads, query_seg, key_seg)
    chance = jnp.exp(scores - summary[..., None])
    rounded = chance.astype(jnp.bfloat16)
    chance_grad = jnp.einsum(
        "qhd,khd->hqk", grad_heads, value_heads, preferred_element_type=jnp.float32
    )
    value_grad = jnp.einsum("hqk,qhd->khd", rounded, grad_heads, preferred_element_type=jnp.float32)
    inner = jnp.sum(chance * chance_grad, axis=-1, keepdims=True)
    score_grad = (chance * (chance_grad - inner)).astype(jnp.bfloat16)
    query_grad = jnp.einsum(
        "hqk,khd->qhd", score_grad, key_heads, preferred_element_type=jnp.float32
    ) * DH ** (-0.5)
    key_grad = jnp.einsum(
        "hqk,qhd->khd", score_grad, query_heads, preferred_element_type=jnp.float32
    ) * DH ** (-0.5)
    return (
        query_grad.reshape(queries.shape[0], width),
        key_grad.reshape(key_rows.shape[0], width),
        value_grad.reshape(key_rows.shape[0], width),
    )


def attention_forward(queries, key_rows, value_rows, query_seg, key_seg):
    return lax.map(
        lambda item: attend_forward(item[0], item[1], item[2], item[3], item[4]),
        (queries, key_rows, value_rows, query_seg, key_seg),
    )


def attention_backward(queries, key_rows, value_rows, context_grad, summary, query_seg, key_seg):
    return lax.map(
        lambda item: attend_backward(item[0], item[1], item[2], item[3], item[4], item[5], item[6]),
        (queries, key_rows, value_rows, context_grad, summary, query_seg, key_seg),
    )


def local(
    hidden_in,
    lengths,
    qkv_weight,
    query_bias,
    value_bias,
    out_weight,
    out_bias,
    gain_one,
    shift_one,
    up_weight,
    up_bias,
    down_weight,
    down_bias,
    gain_two,
    shift_two,
    cotangent,
):
    row_count = hidden_in.shape[0]
    part_len = hidden_in.shape[1]
    flat_in = hidden_in.reshape(row_count * part_len, D)
    hidden = flat_in.astype(jnp.float32)
    joint_weight = qkv_weight.reshape(D, 3, D)
    joint = jnp.einsum("td,dce->cte", flat_in, joint_weight, preferred_element_type=jnp.float32)
    biases = jnp.stack([query_bias, jnp.zeros_like(query_bias), value_bias]).astype(jnp.float32)
    stacked = (joint + biases[:, None, :]).astype(jnp.bfloat16).reshape(3, row_count, part_len, D)
    segment = segment_ids(lengths)
    spread_rows = lax.all_to_all(stacked, "heads", split_axis=3, concat_axis=2, tiled=True)
    context_heads, summary = attention_forward(
        spread_rows[0], spread_rows[1], spread_rows[2], segment, segment
    )
    context = lax.all_to_all(context_heads, "heads", split_axis=1, concat_axis=2, tiled=True)
    context = context.reshape(row_count * part_len, D)
    branch = jnp.dot(context, out_weight, preferred_element_type=jnp.float32) + out_bias.astype(
        jnp.float32
    )
    first, first_back = jax.vjp(
        layer_norm, hidden + branch, gain_one.astype(jnp.float32), shift_one.astype(jnp.float32)
    )
    first_low = first.astype(jnp.bfloat16)
    inner = jnp.dot(first_low, up_weight, preferred_element_type=jnp.float32) + up_bias.astype(
        jnp.float32
    )
    active, gelu_back = jax.vjp(exact_gelu, inner)
    active_low = active.astype(jnp.bfloat16)
    outer = jnp.dot(active_low, down_weight, preferred_element_type=jnp.float32) + down_bias.astype(
        jnp.float32
    )
    final, final_back = jax.vjp(
        layer_norm, first + outer, gain_two.astype(jnp.float32), shift_two.astype(jnp.float32)
    )
    layer_out = final.astype(jnp.bfloat16)
    second_grad, gaintwo_grad, shifttwo_grad = final_back(
        cotangent.reshape(row_count * part_len, D).astype(jnp.float32)
    )
    outer_grad = second_grad.astype(jnp.bfloat16)
    down_grad = jnp.einsum("tf,td->fd", active_low, outer_grad, preferred_element_type=jnp.float32)
    downb_grad = jnp.sum(outer_grad.astype(jnp.float32), axis=0)
    active_grad = jnp.einsum(
        "td,fd->tf", outer_grad, down_weight, preferred_element_type=jnp.float32
    )
    inner_grad = gelu_back(active_grad)[0].astype(jnp.bfloat16)
    up_grad = jnp.einsum("td,tf->df", first_low, inner_grad, preferred_element_type=jnp.float32)
    upb_grad = jnp.sum(inner_grad.astype(jnp.float32), axis=0)
    first_grad = second_grad + jnp.einsum(
        "tf,df->td", inner_grad, up_weight, preferred_element_type=jnp.float32
    )
    residual_grad, gainone_grad, shiftone_grad = first_back(first_grad)
    branch_grad = residual_grad.astype(jnp.bfloat16)
    out_grad = jnp.einsum("te,td->ed", context, branch_grad, preferred_element_type=jnp.float32)
    outb_grad = jnp.sum(branch_grad.astype(jnp.float32), axis=0)
    context_grad = jnp.einsum(
        "td,ed->te", branch_grad, out_weight, preferred_element_type=jnp.float32
    )
    context_grad = context_grad.astype(jnp.bfloat16).reshape(row_count, part_len, D)
    heads_grad = lax.all_to_all(context_grad, "heads", split_axis=2, concat_axis=1, tiled=True)
    query_grad, key_grad, value_grad = attention_backward(
        spread_rows[0], spread_rows[1], spread_rows[2], heads_grad, summary, segment, segment
    )
    stack_heads = jnp.stack([query_grad, key_grad, value_grad]).astype(jnp.bfloat16)
    stack_grad = lax.all_to_all(stack_heads, "heads", split_axis=2, concat_axis=3, tiled=True)
    stack_grad = stack_grad.reshape(3, row_count * part_len, D)
    qkv_grad = jnp.einsum(
        "td,cte->dce", flat_in, stack_grad, preferred_element_type=jnp.float32
    ).reshape(D, 3 * D)
    queryb_grad = jnp.sum(stack_grad[0].astype(jnp.float32), axis=0)
    valueb_grad = jnp.sum(stack_grad[2].astype(jnp.float32), axis=0)
    input_grad = residual_grad + jnp.einsum(
        "cte,dce->td", stack_grad, joint_weight, preferred_element_type=jnp.float32
    )
    rows_total = lengths.shape[0] * lax.axis_size("rows")
    vector_total = lax.psum(
        (
            queryb_grad,
            valueb_grad,
            outb_grad,
            gainone_grad,
            shiftone_grad,
            upb_grad,
            downb_grad,
            gaintwo_grad,
            shifttwo_grad,
        ),
        ("rows", "heads"),
    )
    halfway = (
        lax.psum_scatter(
            qkv_grad.astype(jnp.bfloat16), "heads", scatter_dimension=1, tiled=True
        ).astype(jnp.float32),
        lax.psum_scatter(
            out_grad.astype(jnp.bfloat16), "heads", scatter_dimension=1, tiled=True
        ).astype(jnp.float32),
        lax.psum_scatter(
            up_grad.astype(jnp.bfloat16), "heads", scatter_dimension=1, tiled=True
        ).astype(jnp.float32),
        lax.psum_scatter(
            down_grad.astype(jnp.bfloat16), "heads", scatter_dimension=1, tiled=True
        ).astype(jnp.float32),
    )
    matrix_total = (
        lax.psum_scatter(halfway[0], "rows", scatter_dimension=0, tiled=True),
        lax.psum_scatter(halfway[1], "rows", scatter_dimension=0, tiled=True),
        lax.psum_scatter(halfway[2], "rows", scatter_dimension=0, tiled=True),
        lax.psum_scatter(halfway[3], "rows", scatter_dimension=0, tiled=True),
    )
    mats = [item / rows_total for item in matrix_total]
    vects = [item / rows_total for item in vector_total]
    return (
        layer_out.reshape(row_count, part_len, D),
        input_grad.reshape(row_count, part_len, D),
        mats[0],
        vects[0],
        vects[1],
        mats[1],
        vects[2],
        vects[3],
        vects[4],
        mats[2],
        vects[5],
        mats[3],
        vects[6],
        vects[7],
        vects[8],
    )


def solution(mesh):
    in_specs = (
        P("rows", "heads", None),
        P("rows", None),
        P(),
        P(),
        P(),
        P(),
        P(),
        P(),
        P(),
        P(),
        P(),
        P(),
        P(),
        P(),
        P(),
        P("rows", "heads", None),
    )
    out_specs = (
        P("rows", "heads", None),
        P("rows", "heads", None),
        P("rows", "heads"),
        P(),
        P(),
        P("rows", "heads"),
        P(),
        P(),
        P(),
        P("rows", "heads"),
        P(),
        P("rows", "heads"),
        P(),
        P(),
        P(),
    )
    return jax.shard_map(local, mesh=mesh, in_specs=in_specs, out_specs=out_specs, check_vma=False)
```

profile of v0, /device:TPU:0, one launch (start us, length us, event | category | flops | bytes accessed | tf_op | source)
XLA Modules:
  0.0 872.2 jit_solution(13488707148222625384)
XLA Ops:
  8.7 5.8 copy.100
  14.6 6.3 add_convert_fusion.1
  25.1 5.3 all-to-all-start
  30.6 54.3 %all-to-all-done = bf16[3,8,128,768]{2,1,0,3:T(8,128)(2,1)} async-done(((bf16[3,8,128,768]{2,1,0,3:T(8,128)(2,1)}), bf16[3,8,128,768]{2,1,0,3:T(8,128)(2,1)}, u32[]{:S(2)}, u32[]{:S(2)}) %all-to-all-start) | async-done | bytes 4718624 | tf_op jit(solution)/shard_map/all_to_all | solution.py:129
  108.2 48.9 %while.26 = (s32[]{:T(128)}, bf16[8,512,192]{1,2,0:T(8,128)(2,1)}, f32[8,3,512]{2,1,0:T(4,128)}, bf16[8,512,192]{1,2,0:T(8,128)(2,1)}, s32[8,512]{1,0:T(8,128)S(...) while((s32[]{:T(128)}, bf16[8,512,192]{1,2,0:T(8,128)(2,1)}, ...), condition=%wide.region_5.6_spmd, body=%wide.region_2.5_spmd.sunk | while | flops 211122688 | bytes 12902513 | solution.py:89
  157.2 4.4 copy.105
  161.6 4.4 all-to-all-start.1
  166.5 25.3 %all-to-all-done.1 = bf16[8,512,192]{2,0,1:T(8,128)(2,1)} async-done(((bf16[8,512,192]{2,0,1:T(8,128)(2,1)}), bf16[8,512,192]{2,0,1:T(8,128)(2,1)}, u32[]{:S(2)}, u32[]{:S(2)}) %all-to-all-start.1) | async-done | bytes 1572896 | tf_op jit(solution)/shard_map/all_to_all | solution.py:133
  200.0 35.5 %multiply_convert_fusion.1 = (bf16[1024,3072]{1,0:T(8,128)(2,1)S(1)}, f32[1024,3072]{1,0:T(8,128)}, f32[1024,3072]{1,0:T(8,128)}) fusion(f32[3072]{0:T(1024)S(1)} %convert_element_type.152, bf16[768,3072]{1,0:T(8,128)(2,1)S(1)} %bitcast.228, f32[1024,768]{1,0:T(8,128)S(1)} %get-tuple-element.260, f32[768]{0:T(1024)S(1)} %convert_element_type.150, ...), kind=kOutput, calls=%fused_computation.37 | convolution fusion | flops 5043388416 | bytes 39348224 | tf_op jit(solution)/shard_map/dot_general | solution.py:142
  235.6 5.5 fusion.37
  249.9 18.1 %convert_reduce_fusion = (f32[3072]{0:T(1024)S(1)}, bf16[1024,3072]{1,0:T(8,128)(2,1)}) fusion(f32[1024,3072]{1,0:T(8,128)} %get-tuple-element.246, bf16[1024,768]{1,0:T(8,128)(2,1)} %get-tuple-element.238, bf16[3072,768]{1,0:T(8,128)(2,1)} %param.31, f32[1024,3072]{1,0:T(8,128)} %get-tuple-element.261, f32[3072]{0:T(1024)S(1)} %convert_element_type.152), kind=kOutput, calls=%fused_computation.35 | convolution fusion | flops 4885312512 | bytes 37773312 | tf_op jit(solution)/shard_map/td,fd->tf/dot_general | solution.py:160
  268.1 10.2 %multiply_reduce_fusion.1 = (f32[768]{0:T(1024)S(1)}, f32[1024]{0:T(1024)S(1)}, f32[768]{0:T(1024)S(1)}, f32[1024,768]{1,0:T(8,128)S(1)}) fusion(f32[1024,768]{1,0:T(8,128)S(1)} %get-tuple-element.260, f32[1024]{0:T(1024)S(1)} %fusion.27, f32[1024]{0:T(1024)S(1)} %broadcast_multiply_fusion.14, f32[768]{0:T(1024)S(1)} %convert_element_type.149, ...), kind=kOutput, calls=%fused_computation.66 | convolution fusion | flops 4839699456 | bytes 20472832 | tf_op jit(solution)/shard_map/tf,df->td/dot_general | solution.py:166
  285.5 10.5 %convolution_convert_fusion.1 = bf16[768,3072]{1,0:T(8,128)(2,1)} fusion(bf16[1024,3072]{1,0:T(8,128)(2,1)} %get-tuple-element.266, f32[1024,768]{1,0:T(8,128)} %copy-done.3, f32[768]{0:T(1024)S(1)} %convert_element_type.150, f32[768]{0:T(1024)S(1)} %convert_element_type.149, f32[1024]{0:T(1024)S(1)} %fusion.27, f32[1024]{0:T(1024)S(1)} %broadcast_multiply_fusion.14), kind=kOutput, calls=%fused_computation.54 | convolution fusion | flops 4838129664 | bytes 14170112 | tf_op jit(solution)/shard_map/td,tf->df/dot_general | solution.py:164
  303.1 4.3 all-to-all-start.2
  307.5 9.3 %convolution_convert_fusion = bf16[3072,768]{0,1:T(8,128)(2,1)} fusion(bf16[1024,3072]{1,0:T(8,128)(2,1)} %copy-done.18, bf16[1024,768]{1,0:T(8,128)(2,1)} %get-tuple-element.238), kind=kOutput, calls=%fused_computation.53 | convolution fusion | flops 4834197504 | bytes 12582912 | tf_op jit(solution)/shard_map/tf,td->fd/dot_general | solution.py:158
  317.0 11.5 %all-to-all-done.2 = bf16[8,128,768]{1,0,2:T(8,128)(2,1)} async-done(((bf16[8,128,768]{1,0,2:T(8,128)(2,1)}), bf16[8,128,768]{1,0,2:T(8,128)(2,1)}, u32[]{:S(2)}, u32[]{:S(2)}) %all-to-all-start.2) | async-done | bytes 1572896 | tf_op jit(solution)/shard_map/all_to_all | solution.py:177
  335.9 89.4 %while.27 = (s32[]{:T(128)}, bf16[8,512,192]{1,2,0:T(8,128)(2,1)}, bf16[8,512,192]{1,2,0:T(8,128)(2,1)}, bf16[8,512,192]{1,2,0:T(8,128)(2,1)}, bf16[8,512,192]{1...) while((s32[]{:T(128)}, bf16[8,512,192]{1,2,0:T(8,128)(2,1)}, ...), condition=%wide.region_16.17_spmd, body=%wide.region_14.16_spmd.sunk | while | flops 511048192 | bytes 28872852 | solution.py:96
  425.3 4.4 copy.112
  429.7 4.4 copy.111
  434.1 4.4 copy.110
  442.5 74.2 %all_to_all.63 = bf16[3,8,512,192]{3,1,0,2:T(8,128)(2,1)} all-to-all(bf16[3,8,512,192]{3,1,0,2:T(8,128)(2,1)S(1)} %pad_maximum_fusion), channel_id=1, replica_groups=mesh['rows'=8,'heads'=4] {'heads'}, dimensions={2} | all-to-all | bytes 9437184 | tf_op jit(solution)/shard_map/all_to_all | solution.py:182
  516.7 9.4 %copy.113 = bf16[3,8,4,128,192]{3,1,4,2,0:T(8,128)(2,1)} copy(bf16[3,8,4,128,192]{4,1,0,3,2:T(8,128)(2,1)} %bitcast.201) | data formatting | bytes 9437184 | tf_op jit(solution)/shard_map/all_to_all | solution.py:182
  526.1 8.2 reshape.304
  534.2 8.5 convolution_convert_fusion.2
  551.3 32.2 %reduce-scatter.25.cloned.1.call-done = bf16[576,768]{1,0:T(8,128)(2,1)} async-done(((bf16[2304,768]{1,0:T(8,128)(2,1)}), bf16[576,768]{1,0:T(8,128)(2,1)}) %reduce-scatter.25.cloned.1.call-update) | async-done | bytes 884752
  588.7 60.5 %reduce-scatter.27.cloned.1.call-done = f32[96,192]{1,0:T(8,128)} async-done(((f32[768,192]{1,0:T(8,128)}), f32[96,192]{1,0:T(8,128)}) %reduce-scatter.27.cloned.1.call-update) | async-done | bytes 73744
  650.9 4.9 convert_reduce_fusion.4
  656.0 41.5 %all-reduce = (f32[768]{0:T(1024)S(1)}, f32[768]{0:T(1024)S(1)}, f32[768]{0:T(1024)S(1)}, f32[768]{0:T(1024)S(1)}, f32[768]{0:T(1024)S(1)}, /*index=5*/f32[3072]...) all-reduce(f32[768]{0:T(1024)S(1)} %reduce_sum.226, ...), channel_id=1, replica_groups=mesh['rows'=8,'heads'=4] {'rows','heads'}, use_global_device_ids=true, to_apply=%region_20.21 | all-reduce | flops 9216 | bytes 73728 | tf_op jit(solution)/shard_map/psum | solution.py:193
  700.5 9.9 %bitcast_add_fusion = f32[1024,768]{1,0:T(8,128)} fusion(f32[1024,768]{1,0:T(8,128)} %copy-done.2, bf16[3,1024,768]{1,2,0:T(8,128)(2,1)} %reshape.304, bf16[768,3,768]{0,2,1:T(8,128)(2,1)} %bitcast.216, f32[1024]{0:T(1024)S(1)} %negate_multiply_fusion.1), kind=kOutput, calls=%fused_computation.57 | convolution fusion | flops 3625451520 | bytes 14553088 | tf_op jit(solution)/shard_map/cte,dce->td/dot_general | solution.py:189
  710.4 11.2 %reduce-scatter.19.cloned.1.call-done = f32[96,768]{1,0:T(8,128)} async-done(((f32[768,768]{1,0:T(8,128)}), f32[96,768]{1,0:T(8,128)}) %reduce-scatter.19.cloned.1.call-update) | async-done | bytes 294928 | tf_op jit(solution)/shard_map/reduce_scatter | solution.py:224
  723.3 70.3 %reduce-scatter.23.cloned.1.call-done = f32[384,192]{0,1:T(8,128)} async-done(((f32[3072,192]{0,1:T(8,128)}), f32[384,192]{0,1:T(8,128)}) %reduce-scatter.23.cloned.1.call-update) | async-done | bytes 294928 | tf_op jit(solution)/shard_map/reduce_scatter | solution.py:225
  795.2 68.1 %reduce-scatter.13.cloned.1.call-done = f32[96,576]{1,0:T(8,128)} async-done(((f32[768,576]{1,0:T(8,128)}), f32[96,576]{1,0:T(8,128)}) %reduce-scatter.13.cloned.1.call-update) | async-done | bytes 221200 | tf_op jit(solution)/shard_map/reduce_scatter | solution.py:222
  (328 shorter events, 233.7 us)
Async XLA Ops:
  7.2 188.5 %copy-start = (bf16[768,768]{1,0:T(8,128)(2,1)S(1)}, bf16[768,768]{1,0:T(8,128)(2,1)}, u32[]{:S(2)}) copy-start(bf16[768,768]{1,0:T(8,128)(2,1)} %param.25) | copy-start | bytes 3538948
  25.1 5.3 copy-start.17
  25.1 59.7 %all-to-all-start = ((bf16[3,8,128,768]{2,1,0,3:T(8,128)(2,1)}), bf16[3,8,128,768]{2,1,0,3:T(8,128)(2,1)}, u32[]{:S(2)}, u32[]{:S(2)}) async-start(bf16[3,8,128,768]{2,1,0,3:T(8,128)(2,1)} %copy.101), calls=%async_computation | async-start | bytes 9437184 | tf_op jit(solution)/shard_map/all_to_all | solution.py:129
  157.1 4.5 copy-start.8
  157.1 9.3 %copy-start.11 = (bf16[768]{0:T(1024)(128)(2,1)S(1)}, bf16[768]{0:T(1024)(128)(2,1)}, u32[]{:S(2)}) copy-start(bf16[768]{0:T(1024)(128)(2,1)} %param.32) | copy-start | bytes 4612
  157.1 9.3 %copy-start.10 = (bf16[3072]{0:T(1024)(128)(2,1)S(1)}, bf16[3072]{0:T(1024)(128)(2,1)}, u32[]{:S(2)}) copy-start(bf16[3072]{0:T(1024)(128)(2,1)} %param.30) | copy-start | bytes 18436
  157.1 9.3 %copy-start.12 = (bf16[768]{0:T(1024)(128)(2,1)S(1)}, bf16[768]{0:T(1024)(128)(2,1)}, u32[]{:S(2)}) copy-start(bf16[768]{0:T(1024)(128)(2,1)} %param.26) | copy-start | bytes 4612
  157.1 9.3 %copy-start.13 = (bf16[768]{0:T(1024)(128)(2,1)S(1)}, bf16[768]{0:T(1024)(128)(2,1)}, u32[]{:S(2)}) copy-start(bf16[768]{0:T(1024)(128)(2,1)} %param.28) | copy-start | bytes 4612
  157.1 9.3 %copy-start.14 = (bf16[768]{0:T(1024)(128)(2,1)S(1)}, bf16[768]{0:T(1024)(128)(2,1)}, u32[]{:S(2)}) copy-start(bf16[768]{0:T(1024)(128)(2,1)} %param.27) | copy-start | bytes 4612
  157.2 9.3 %copy-start.15 = (bf16[768]{0:T(1024)(128)(2,1)S(1)}, bf16[768]{0:T(1024)(128)(2,1)}, u32[]{:S(2)}) copy-start(bf16[768]{0:T(1024)(128)(2,1)} %param.33) | copy-start | bytes 4612
  157.2 9.3 %copy-start.16 = (bf16[768]{0:T(1024)(128)(2,1)S(1)}, bf16[768]{0:T(1024)(128)(2,1)}, u32[]{:S(2)}) copy-start(bf16[768]{0:T(1024)(128)(2,1)} %param.34) | copy-start | bytes 4612
  161.6 30.2 %all-to-all-start.1 = ((bf16[8,512,192]{2,0,1:T(8,128)(2,1)}), bf16[8,512,192]{2,0,1:T(8,128)(2,1)}, u32[]{:S(2)}, u32[]{:S(2)}) async-start(bf16[8,512,192]{2,0,1:T(8,128)(2,1)} %copy.105), calls=%async_computation.1 | async-start | bytes 4194304 | tf_op jit(solution)/shard_map/all_to_all | solution.py:133
  166.1 376.7 %reduce-scatter.15.cloned.1.call-start = ((), (), s32[]{:S(2)}) async-start(), calls=%async_computation.13 | async-start | bytes 1474560 | tf_op jit(solution)/shard_map/reduce_scatter | solution.py:211
  195.7 3.7 copy-start.5
  195.7 4.3 slice-start.2
  195.7 4.3 slice-start.3
  195.7 39.8 %slice-start = ((s8[4718592]{0:T(1024)(128)(4,1)}), s8[4194304]{0:T(1024)(128)(4,1)S(1)}, s32[]{:S(2)}) async-start(s8[4718592]{0:T(1024)(128)(4,1)} %bitcast.225), calls=%async_computation.20 | async-start | bytes 8388608
  199.4 78.8 %copy-start.3 = (f32[1024,768]{1,0:T(8,128)}, f32[1024,768]{1,0:T(8,128)S(1)}, u32[]{:S(2)}) copy-start(f32[1024,768]{1,0:T(8,128)S(1)} %get-tuple-element.260) | copy-start | bytes 9437188
  200.0 35.5 %slice-start.1 = ((s8[4718592]{0:T(1024)(128)(4,1)}), s8[524288]{0:T(1024)(128)(4,1)S(1)}, s32[]{:S(2)}) async-start(s8[4718592]{0:T(1024)(128)(4,1)} %bitcast.225), calls=%async_computation.21 | async-start | bytes 1048576
  235.5 5.5 copy-start.18
  246.8 1.7 copy-start.4
  279.8 1.7 copy-start.2
  279.8 3.2 copy-start.6
  285.5 259.4 %reduce-scatter.17.cloned.1.call-start = ((), (), s32[]{:S(2)}) async-start(), calls=%async_computation.14 | async-start | bytes 5898240 | tf_op jit(solution)/shard_map/reduce_scatter | solution.py:214
  303.1 25.4 %all-to-all-start.2 = ((bf16[8,128,768]{1,0,2:T(8,128)(2,1)}), bf16[8,128,768]{1,0,2:T(8,128)(2,1)}, u32[]{:S(2)}, u32[]{:S(2)}) async-start(bf16[8,128,768]{1,0,2:T(8,128)(2,1)} %copy.107), calls=%async_computation.2 | async-start | bytes 3145728 | tf_op jit(solution)/shard_map/all_to_all | solution.py:177
  307.4 240.7 %reduce-scatter.21.cloned.1.call-start = ((), (), s32[]{:S(2)}) async-start(), calls=%async_computation.16 | async-start | bytes 5898240 | tf_op jit(solution)/shard_map/reduce_scatter | solution.py:217
  316.7 266.8 %reduce-scatter.25.cloned.1.call-start = ((), (), s32[]{:S(2)}) async-start(), calls=%async_computation.18 | async-start | bytes 4423680
  542.7 106.5 %reduce-scatter.27.cloned.1.call-start = ((), (), s32[]{:S(2)}) async-start(), calls=%async_computation.19 | async-start | bytes 884736
  544.8 176.7 %reduce-scatter.19.cloned.1.call-start = ((), (), s32[]{:S(2)}) async-start(), calls=%async_computation.15 | async-start | bytes 2654208 | tf_op jit(solution)/shard_map/reduce_scatter | solution.py:224
  547.8 245.7 %reduce-scatter.23.cloned.1.call-start = ((), (), s32[]{:S(2)}) async-start(), calls=%async_computation.17 | async-start | bytes 2654208 | tf_op jit(solution)/shard_map/reduce_scatter | solution.py:225
  551.2 312.0 %reduce-scatter.13.cloned.1.call-start = ((), (), s32[]{:S(2)}) async-start(), calls=%async_computation.12 | async-start | bytes 2211840 | tf_op jit(solution)/shard_map/reduce_scatter | solution.py:222
  588.4 67.6 %copy-start.9 = (f32[768]{0:T(1024)S(1)}, f32[768]{0:T(1024)}, u32[]{:S(2)}) copy-start(f32[768]{0:T(1024)} %get-tuple-element.189) | copy-start | bytes 9220
  (2 other events, 2.6 us)
Sparse Core Ops, SparseCore 0:
  285.6 27.8 reduce-scatter.14
  316.2 46.8 reduce-scatter.16
  365.6 47.8 reduce-scatter.20
  542.8 40.6 reduce-scatter.24
  586.7 62.4 reduce-scatter.26
  652.9 68.5 reduce-scatter.18
  725.5 68.0 reduce-scatter.22
  797.4 65.8 reduce-scatter.12
where the time goes:
time: 881 us; the launch traced here: 872 us
  waiting for transfers between devices  334 us (38%)
  local copies, waits for them, and re-layouts  171 us (19%)
  matrix products  166 us (19%)
  blocking collectives  116 us (13%)
  other arithmetic  55.3 us (6%)
  between operations  15.2 us (2%)
  starting transfers between devices  15.1 us (2%)
    unnamed x10, waiting for transfers between devices  92.9 us
    all_to_all x1, blocking collectives, local(): lax.all_to_all(stack_heads, 'heads', split_axis=2, concat_axis=3, tiled=T...  74.2 us
    reduce_scatter x1, waiting for transfers between devices, local(): lax.psum_scatter(halfway[3], 'rows', scatter_dimension=0, tiled=True)  70.3 us
    reduce_scatter x1, waiting for transfers between devices, local(): lax.psum_scatter(halfway[0], 'rows', scatter_dimension=0, tiled=True)  68.1 us
    all_to_all x1, waiting for transfers between devices, local(): lax.all_to_all(stacked, 'heads', split_axis=3, concat_axis=2, tiled=True)  54.3 us
    dynamic_slice x64, local copies, waits for them, and re-layouts, attention_forward(): lax.map(lambda item: attend_forward(item[0], item[1], item[2], item[3], i...  52.4 us
    psum x1, blocking collectives, local(): lax.psum((queryb_grad, valueb_grad, outb_grad, gainone_grad, shiftone_gra...  41.5 us
    dot_general x1, matrix products, local(): jnp.dot(first_low, up_weight, preferred_element_type=jnp.float32)  35.5 us
  transfers between devices with their start and end apart: 11, of which 8 were waited for; matrix products, arithmetic and copies ran while one was open for 23% of the time, Pallas kernels for 0%

commit v1 on v0

v1 whole, which is shorter than its diff:
```python
import functools

import jax
import jax.numpy as jnp
from jax import lax
from jax.experimental import pallas as pl
from jax.experimental.pallas import tpu as pltpu
from jax.sharding import PartitionSpec as P

DH = 64
D = 768
L = 512
EPSILON = 1e-12
OFF = -(2.0**100)
F32 = jnp.float32
BF16 = jnp.bfloat16
NN = (((1,), (0,)), ((), ()))
NT = (((1,), (1,)), ((), ()))
TN = (((0,), (0,)), ((), ()))

TAIL = (
    0.09881087227319621,
    0.11230449770687516,
    0.02424904968806795,
    0.2825055677430211,
    -0.268648558796486,
    0.34262844642428514,
    -0.09184987882933851,
)


def mm(left, right, dims=NN):
    return lax.dot_general(left, right, dims, preferred_element_type=F32)


def normal_parts(u):
    bell = jnp.exp(u * u * -0.5)
    t = pltpu.reciprocal(1.0 + 0.25 * jnp.abs(u))
    poly = TAIL[-1]
    for item in TAIL[-2::-1]:
        poly = poly * t + item
    tail = poly * t * bell
    return jnp.where(u >= 0, 1.0 - tail, tail), bell * 0.3989422804014327


def norm_parts(values):
    middle = jnp.mean(values, axis=-1, keepdims=True)
    center = values - middle
    spread = jnp.mean(center * center, axis=-1, keepdims=True)
    scale = lax.rsqrt(spread + EPSILON)
    return center * scale, scale


def norm_back(grad, normed, scale, gain):
    dn = grad * gain
    first = jnp.mean(dn, axis=-1, keepdims=True)
    second = jnp.mean(dn * normed, axis=-1, keepdims=True)
    return (dn - first - normed * second) * scale


def split3(values):
    high = values.astype(BF16)
    rest = values - high.astype(F32)
    mid = rest.astype(BF16)
    return high, mid, (rest - mid.astype(F32)).astype(BF16)


def features(ends, key_feat, query_feat, start):
    token = lax.broadcasted_iota(jnp.int32, (L, 128), 0)
    place = lax.broadcasted_iota(jnp.int32, (L, 128), 1) & (DH - 1)
    seg = jnp.zeros((L, 128), jnp.int32)
    for end in ends:
        seg = seg + (token >= end).astype(jnp.int32)
    count = len(ends)
    ones = (place == seg) | ((place >= count) & (place < count + 3))
    key_feat[pl.ds(start, L), :] = jnp.where(ones, 1.0, 0.0).astype(BF16)
    off = (place < count) & (place != seg)
    query_feat[pl.ds(start, L), :] = jnp.where(off, OFF, 0.0).astype(BF16)


def attend(rows, group, pairs, qkv, ctx, lse, key_feat, query_feat):
    lane = lax.broadcasted_iota(jnp.int32, (1, 128), 1)
    kf, qf = key_feat[rows, :], query_feat[rows, :]
    ops, values = [], []
    for pair in range(pairs):
        col = pl.multiple_of(group * (pairs * 128) + pair * 128, 128)
        q2 = qkv[rows, pl.ds(col, 128)]
        k2 = qkv[rows, pl.ds(D + col, 128)]
        values.append(qkv[rows, pl.ds(2 * D + col, 128)])
        for own in (lane < DH, lane >= DH):
            ops.append((jnp.where(own, q2, qf), jnp.where(own, k2, kf)))
    count = 2 * pairs
    scores = [None] * count
    outs, sums = [], []
    scores[0] = mm(*ops[0], NT)
    for head in range(count):
        if head + 1 < count:
            scores[head + 1] = mm(*ops[head + 1], NT)
        peak = jnp.max(scores[head], axis=1, keepdims=True)
        expo = jnp.exp(scores[head] - peak)
        total = jnp.sum(expo, axis=1, keepdims=True)
        out = mm(expo.astype(BF16), values[head // 2])
        outs.append(out * (1.0 / total))
        sums.append(peak + jnp.log(total))
    keep = jnp.zeros((L, 128), F32)
    for head in range(count):
        keep = jnp.where(lane == head, sums[head], keep)
    lse[group, rows, :] = keep
    for pair in range(pairs):
        col = pl.multiple_of(group * (pairs * 128) + pair * 128, 128)
        both = jnp.where(lane < DH, outs[2 * pair], outs[2 * pair + 1])
        ctx[rows, pl.ds(col, 128)] = both.astype(BF16)


def attend_back(rows, group, pairs, qkv, ctx, dctx, lse, grads, key_feat, query_feat):
    lane = lax.broadcasted_iota(jnp.int32, (1, 128), 1)
    place = lane & (DH - 1)
    kf, qf = key_feat[rows, :], query_feat[rows, :]
    vf = jnp.where((place >= 4) & (place < 7), 1.0, 0.0).astype(BF16)
    keep = lse[group, rows, :]

    def spread(column, base):
        high, mid, small = split3(-column)
        return jnp.where(
            place == 4, high, jnp.where(place == 5, mid, jnp.where(place == 6, small, base))
        )

    ops = []
    for pair in range(pairs):
        col = pl.multiple_of(group * (pairs * 128) + pair * 128, 128)
        q2 = qkv[rows, pl.ds(col, 128)]
        k2 = qkv[rows, pl.ds(D + col, 128)]
        v2 = qkv[rows, pl.ds(2 * D + col, 128)]
        d2 = dctx[rows, pl.ds(col, 128)]
        both = d2.astype(F32) * ctx[rows, pl.ds(col, 128)].astype(F32)
        zero = jnp.zeros_like(q2)
        for side, own in enumerate((lane < DH, lane >= DH)):
            inner = jnp.sum(jnp.where(own, both, 0.0), axis=1, keepdims=True)
            total = keep[:, 2 * pair + side : 2 * pair + side + 1]
            ops.append(
                (
                    jnp.where(own, k2, kf),
                    jnp.where(own, q2, spread(total, qf)),
                    jnp.where(own, v2, vf),
                    jnp.where(own, d2, spread(inner, zero)),
                    jnp.where(own, q2, zero),
                    jnp.where(own, k2, zero),
                    jnp.where(own, d2, zero),
                )
            )
    count = 2 * pairs
    scores, chances = [None] * count, [None] * count
    dq, dk, dv = [0] * pairs, [0] * pairs, [0] * pairs

    def start(head):
        scores[head] = mm(ops[head][0], ops[head][1], NT)
        chances[head] = mm(ops[head][2], ops[head][3], NT)

    start(0)
    for head in range(count):
        if head + 1 < count:
            start(head + 1)
        chance = jnp.exp(scores[head])
        low = chance.astype(BF16)
        ds = (chance * chances[head]).astype(BF16)
        pair = head // 2
        dk[pair] += mm(ds, ops[head][4])
        dv[pair] += mm(low, ops[head][6])
        dq[pair] += mm(ds, ops[head][5], TN)
    for pair in range(pairs):
        col = pl.multiple_of(group * (pairs * 128) + pair * 128, 128)
        grads[rows, pl.ds(col, 128)] = (dq[pair] * DH**-0.5).astype(BF16)
        grads[rows, pl.ds(D + col, 128)] = dk[pair].astype(BF16)
        grads[rows, pl.ds(2 * D + col, 128)] = dv[pair].astype(BF16)


def first_kernel(x, lens, wqkv, bqkv, wout, bout, qkv, ctx, r1, lse, key_feat, query_feat):
    for row in range(x.shape[0] // L):
        ends, total = [], 0
        for item in range(lens.shape[1]):
            total = total + lens[row, item]
            ends.append(total)
        features(ends, key_feat, query_feat, row * L)

        rows = pl.ds(row * L, L)
        for part in range(3):
            cols = pl.ds(part * D, D)
            acc = mm(x[rows, :], wqkv[:, cols]) + bqkv[:, cols]
            if part == 0:
                acc = acc * DH**-0.5
            qkv[rows, cols] = acc.astype(BF16)

        def heads(group, carry):
            attend(rows, group, 3, qkv, ctx, lse, key_feat, query_feat)
            return carry

        lax.fori_loop(0, 2, heads, 0)
        r1[rows, :] = mm(ctx[rows, :], wout[...]) + bout[...] + x[rows, :].astype(F32)


def middle_kernel(
    r1, ctx, cot, vecs, wup, bup, wdown, wout,
    y, dr1, dctx, downg, upg, outg, vec_grads, upb_grad,
    fb, act, slope, acc, dfb, dab,
):
    tokens = r1.shape[0]
    step = 256
    parts = tokens // step
    width = 768
    chunks = wup.shape[1] // width
    g1, s1, g2, s2, bd = (vecs[i : i + 1, :] for i in range(5))
    vec_grads[...] = jnp.zeros_like(vec_grads)
    upb_grad[...] = jnp.zeros_like(upb_grad)

    def lead(i, carry):
        rows = pl.ds(pl.multiple_of(i * step, step), step)
        normed, _ = norm_parts(r1[rows, :])
        first = normed * g1 + s1
        fb[rows, :] = first.astype(BF16)
        acc[rows, :] = first + bd
        return carry

    lax.fori_loop(0, parts, lead, 0)

    def forward(c, carry):
        cols = pl.ds(pl.multiple_of(c * width, width), width)
        u, e = [None] * parts, [None] * parts
        for s in range(parts + 2):
            if s < parts:
                u[s] = mm(fb[s * step : (s + 1) * step, :], wup[:, cols]) + bup[:, cols]
            if 0 <= s - 1 < parts:
                j = s - 1
                rows = slice(j * step, (j + 1) * step)
                cdf, pdf = normal_parts(u[j])
                e[j] = (u[j] * cdf).astype(BF16)
                act[rows, cols] = e[j]
                slope[rows, cols] = (cdf + u[j] * pdf).astype(BF16)
            if 0 <= s - 2 < parts:
                j = s - 2
                acc[j * step : (j + 1) * step, :] += mm(e[j], wdown[cols, :])
        return carry

    lax.fori_loop(0, chunks, forward, 0)

    def second(i, carry):
        rows = pl.ds(pl.multiple_of(i * step, step), step)
        normed, scale = norm_parts(acc[rows, :])
        y[rows, :] = (normed * g2 + s2).astype(BF16)
        dy = cot[rows, :].astype(F32)
        dr2 = norm_back(dy, normed, scale, g2)
        acc[rows, :] = dr2
        low = dr2.astype(BF16)
        dfb[rows, :] = low
        vec_grads[0:1, :] += jnp.sum(dy * normed, axis=0, keepdims=True)
        vec_grads[1:2, :] += jnp.sum(dy, axis=0, keepdims=True)
        vec_grads[2:3, :] += jnp.sum(low.astype(F32), axis=0, keepdims=True)
        return carry

    lax.fori_loop(0, parts, second, 0)

    def down(c, carry):
        cols = pl.ds(pl.multiple_of(c * width, width), width)
        downg[:, cols] = mm(dfb[...], act[:, cols], TN).astype(BF16)
        return carry

    lax.fori_loop(0, chunks, down, 0)

    def backward(c, carry):
        cols = pl.ds(pl.multiple_of(c * width, width), width)
        de, du = [None] * parts, [None] * parts
        sums = jnp.zeros((1, width), F32)
        for s in range(parts + 2):
            if s < parts:
                de[s] = mm(dfb[s * step : (s + 1) * step, :], wdown[cols, :], NT)
            if 0 <= s - 1 < parts:
                j = s - 1
                rows = slice(j * step, (j + 1) * step)
                du[j] = (de[j] * slope[rows, cols].astype(F32)).astype(BF16)
                slope[rows, cols] = du[j]
                sums = sums + jnp.sum(du[j].astype(F32), axis=0, keepdims=True)
            if 0 <= s - 2 < parts:
                j = s - 2
                acc[j * step : (j + 1) * step, :] += mm(du[j], wup[:, cols], NT)
        upb_grad[:, cols] = sums
        return carry

    lax.fori_loop(0, chunks, backward, 0)

    def third(i, carry):
        rows = pl.ds(pl.multiple_of(i * step, step), step)
        normed, scale = norm_parts(r1[rows, :])
        grad = acc[rows, :]
        dr = norm_back(grad, normed, scale, g1)
        dr1[rows, :] = dr
        low = dr.astype(BF16)
        dab[rows, :] = low
        vec_grads[3:4, :] += jnp.sum(grad * normed, axis=0, keepdims=True)
        vec_grads[4:5, :] += jnp.sum(grad, axis=0, keepdims=True)
        vec_grads[5:6, :] += jnp.sum(low.astype(F32), axis=0, keepdims=True)
        return carry

    lax.fori_loop(0, parts, third, 0)
    dctx[...] = mm(dab[...], wout[...], NT).astype(BF16)
    outg[...] = mm(ctx[...], dab[...], TN).astype(BF16)

    def up(c, carry):
        cols = pl.ds(pl.multiple_of(c * width, width), width)
        upg[:, cols] = mm(fb[...], slope[:, cols], TN).astype(BF16)
        return carry

    lax.fori_loop(0, chunks, up, 0)


def last_kernel(x, lens, qkv, ctx, dctx, lse, dr1, wqkv, xg, qkvg, vec_grads, grads, key_feat, query_feat):
    vec_grads[...] = jnp.zeros_like(vec_grads)
    for row in range(x.shape[0] // L):
        ends, total = [], 0
        for item in range(lens.shape[1]):
            total = total + lens[row, item]
            ends.append(total)
        features(ends, key_feat, query_feat, row * L)

        rows = pl.ds(row * L, L)

        def heads(group, carry):
            attend_back(rows, group, 3, qkv, ctx, dctx, lse, grads, key_feat, query_feat)
            return carry

        lax.fori_loop(0, 2, heads, 0)
    vec_grads[0:1, :] = jnp.sum(grads[:, 0:D].astype(F32), axis=0, keepdims=True)
    vec_grads[1:2, :] = jnp.sum(grads[:, 2 * D : 3 * D].astype(F32), axis=0, keepdims=True)
    for part in range(3):
        cols = slice(part * D, (part + 1) * D)
        qkvg[:, cols] = mm(x[...], grads[:, cols], TN).astype(BF16)
    xg[...] = (mm(grads[...], wqkv[...], NT) + dr1[...]).astype(xg.dtype)


VMEM = pl.BlockSpec(memory_space=pltpu.VMEM)
SMEM = pl.BlockSpec(memory_space=pltpu.SMEM)


def shape(dims, kind):
    return jax.ShapeDtypeStruct(dims, kind)


def params(**more):
    return pltpu.CompilerParams(vmem_limit_bytes=63 * 2**20, **more)


def local(
    hidden_in, lengths, qkv_weight, query_bias, value_bias, out_weight, out_bias, gain_one,
    shift_one, up_weight, up_bias, down_weight, down_bias, gain_two, shift_two, cotangent,
):
    row_count, part_len = hidden_in.shape[0], hidden_in.shape[1]
    heads = lax.axis_size("heads")
    mine = row_count // heads
    tokens = mine * L
    ff = up_weight.shape[1]
    place = lax.axis_index("heads")
    x = lax.all_to_all(hidden_in, "heads", split_axis=0, concat_axis=1, tiled=True).reshape(tokens, D)
    cot = lax.all_to_all(cotangent, "heads", split_axis=0, concat_axis=1, tiled=True).reshape(tokens, D)
    lens = lax.dynamic_slice_in_dim(lengths, place * mine, mine, 0)
    bqkv = jnp.concatenate([query_bias, jnp.zeros_like(query_bias), value_bias]).astype(F32)[None]
    qkv, ctx, r1, lse = pl.pallas_call(
        first_kernel,
        out_shape=(
            shape((tokens, 3 * D), BF16), shape((tokens, D), BF16), shape((tokens, D), F32),
            shape((2, tokens, 128), F32),
        ),
        in_specs=[VMEM, SMEM] + [VMEM] * 4,
        out_specs=(VMEM,) * 4,
        scratch_shapes=[pltpu.VMEM((tokens, 128), BF16)] * 2,
        compiler_params=params(),
        name="first",
    )(x, lens, qkv_weight, bqkv, out_weight, out_bias.astype(F32)[None])
    vecs = jnp.stack([gain_one, shift_one, gain_two, shift_two, down_bias]).astype(F32)
    y, dr1, dctx, downg, upg, outg, vec_mid, upb = pl.pallas_call(
        middle_kernel,
        out_shape=(
            shape((tokens, D), BF16), shape((tokens, D), F32), shape((tokens, D), BF16),
            shape((D, ff), BF16), shape((D, ff), BF16), shape((D, D), BF16),
            shape((8, D), F32), shape((1, ff), F32),
        ),
        in_specs=[VMEM] * 8,
        out_specs=(VMEM,) * 8,
        scratch_shapes=[
            pltpu.VMEM((tokens, D), BF16), pltpu.VMEM((tokens, ff), BF16), pltpu.VMEM((tokens, ff), BF16),
            pltpu.VMEM((tokens, D), F32), pltpu.VMEM((tokens, D), BF16), pltpu.VMEM((tokens, D), BF16),
        ],
        compiler_params=params(),
        name="middle",
    )(r1, ctx, cot, vecs, up_weight, up_bias.astype(F32)[None], down_weight, out_weight)
    xg, qkvg, vec_last = pl.pallas_call(
        last_kernel,
        out_shape=(shape((tokens, D), BF16), shape((D, 3 * D), BF16), shape((8, D), F32)),
        in_specs=[VMEM, SMEM] + [VMEM] * 6,
        out_specs=(VMEM,) * 3,
        scratch_shapes=[pltpu.VMEM((tokens, 3 * D), BF16)] + [pltpu.VMEM((tokens, 128), BF16)] * 2,
        compiler_params=params(),
        name="last",
    )(x, lens, qkv, ctx, dctx, lse, dr1, qkv_weight)

    def back(values):
        values = values.reshape(mine, L, D)
        return lax.all_to_all(values, "heads", split_axis=1, concat_axis=0, tiled=True)

    layer_out = back(y)
    input_grad = back(xg).astype(F32)
    scale = 1.0 / (row_count * lax.axis_size("rows"))
    vec_mid, vec_last, upb = lax.psum((vec_mid, vec_last, upb), ("rows", "heads"))

    def reduce(values, flip):
        one, two = (0, 1) if flip else (1, 0)
        half = lax.psum_scatter(values, "heads", scatter_dimension=one, tiled=True).astype(F32)
        total = lax.psum_scatter(half, "rows", scatter_dimension=two, tiled=True) * scale
        return total.T if flip else total

    vm, vl = vec_mid * scale, vec_last * scale
    return (
        layer_out, input_grad, reduce(qkvg, False), vl[0], vl[1], reduce(outg, False), vm[5], vm[3], vm[4],
        reduce(upg, False), upb[0] * scale, reduce(downg, True), vm[2], vm[0], vm[1],
    )


def solution(mesh):
    split = P("rows", "heads", None)
    grid = P("rows", "heads")
    in_specs = (split, P("rows", None)) + (P(),) * 13 + (split,)
    out_specs = (split, split, grid, P(), P(), grid, P(), P(), P(), grid, P(), grid, P(), P(), P())
    return jax.shard_map(local, mesh=mesh, in_specs=in_specs, out_specs=out_specs, check_vma=False)
```

time: 881 us -> 620 us (0.70)
  matrix products: 166 us -> 0 us
  local copies, waits for them, and re-layouts: 171 us -> 26.3 us
  Pallas kernels: 0 us -> 117 us
  other arithmetic: 55.3 us -> 18.3 us
  blocking collectives: 116 us -> 79.7 us
  waiting for transfers between devices: 334 us -> 344 us
    dot_general x68 -> x0, matrix products: 166 us -> none  [the longest x1 35.5 us: local(): jnp.dot(first_low, up_weight, preferred_element_type=jnp.float32)]
    reduce_scatter x6, waiting for transfers between devices: 150 us -> 272 us  [the longest x4 177 us: reduce(): lax.psum_scatter(half, 'rows', scatter_dimension=two, tiled=True) * scale]
    pallas_call x0 -> x3, Pallas kernels: none -> 117 us  [the longest x1 61.2 us: local(): pl.pallas_call(middle_kernel, out_shape=(shape((tokens, D), BF16), shape(...]
    all_to_all x3, waiting for transfers between devices: 91.1 us -> 32.7 us  [the longest x2 17.3 us: back(): lax.all_to_all(values, 'heads', split_axis=1, concat_axis=0, tiled=True)]
    unnamed x10, waiting for transfers between devices: 92.9 us -> 39.5 us
    dynamic_slice x64 -> x1, local copies, waits for them, and re-layouts: 52.4 us -> 0.07 us  [local(): lens = lax.dynamic_slice_in_dim(lengths, place * mine, mine, 0)]
    all_to_all x1, blocking collectives: 74.2 us -> 24.3 us  [local(): lax.all_to_all(hidden_in, 'heads', split_axis=0, concat_axis=1, tiled=True)]
    reduce_sum x18 -> x0, other arithmetic: 19.7 us -> none  [the longest x8 5.73 us: attend_forward(): totals = jnp.sum(expos, axis=-1, keepdims=True)]
  transfers between devices with their start and end apart: 11 -> 11, of which waited for: 8 -> 8; matrix products, arithmetic and copies ran while one was open for 23% -> 6% of each run, Pallas kernels for 0% -> 6%
where the time goes in v1:
time: 620 us; the launch traced here: 612 us
  waiting for transfers between devices  344 us (55%)
  Pallas kernels  117 us (19%)
  blocking collectives  79.7 us (13%)
  local copies, waits for them, and re-layouts  26.3 us (4%)
  other arithmetic  18.3 us (3%)
  between operations  14.9 us (2%)
  starting transfers between devices  11.3 us (2%)
    reduce_scatter x4, waiting for transfers between devices, reduce(): lax.psum_scatter(half, 'rows', scatter_dimension=two, tiled=True) * scale  177 us
    reduce_scatter x2, waiting for transfers between devices, reduce(): lax.psum_scatter(values, 'heads', scatter_dimension=one, tiled=True)  94.8 us
    pallas_call x1, Pallas kernels, local(): pl.pallas_call(middle_kernel, out_shape=(shape((tokens, D), BF16), shape(...  61.2 us
    psum x1, blocking collectives, local(): lax.psum((vec_mid, vec_last, upb), ('rows', 'heads'))  55.4 us
    unnamed x10, waiting for transfers between devices  39.5 us
    pallas_call x1, Pallas kernels, local(): pl.pallas_call(last_kernel, out_shape=(shape((tokens, D), BF16), shape((D...  36.1 us
    all_to_all x1, blocking collectives, local(): lax.all_to_all(hidden_in, 'heads', split_axis=0, concat_axis=1, tiled=True)  24.3 us
    pallas_call x1, Pallas kernels, local(): pl.pallas_call(first_kernel, out_shape=(shape((tokens, 3 * D), BF16), sha...  19.8 us
  transfers between devices with their start and end apart: 11, of which 8 were waited for; matrix products, arithmetic and copies ran while one was open for 6% of the time, Pallas kernels for 6%

profile of v1, /device:TPU:0, one launch (start us, length us, event | category | flops | bytes accessed | tf_op | source)
XLA Modules:
  0.0 611.8 jit_solution(850097150968704283)
XLA Ops:
  7.2 24.3 %all_to_all.57 = bf16[8,128,768]{2,1,0:T(8,128)(2,1)S(1)} all-to-all(bf16[8,128,768]{2,1,0:T(8,128)(2,1)} %param.16), channel_id=1, replica_groups=mesh['rows'=8,'heads'=4] {'heads'}, dimensions={0} | all-to-all | bytes 3145728 | tf_op jit(solution)/shard_map/all_to_all | solution.py:360
  31.6 3.7 all-to-all-start.1
  39.9 15.4 %all-to-all-done.1 = bf16[8,128,768]{2,1,0:T(8,128)(2,1)S(1)} async-done(((bf16[8,128,768]{2,1,0:T(8,128)(2,1)}), bf16[8,128,768]{2,1,0:T(8,128)(2,1)S(1)}, u32[]{:S(2)}, u32[]{:S(2)}) %all-to-all-start.1) | async-done | bytes 1572896 | tf_op jit(solution)/shard_map/all_to_all | solution.py:361
  55.3 1.3 copy.38
  56.6 19.8 %first.1 = (bf16[1024,2304]{1,0:T(8,128)(2,1)}, bf16[1024,768]{1,0:T(8,128)(2,1)}, f32[1024,768]{1,0:T(8,128)}, f32[2,1024,128]{2,1,0:T(8,128)}) custom-call(bf16[1024,768]{1,0:T(8,128)(2,1)} %bitcast.28, s32[2,4]{1,0:T(2,128)} %copy.47.lens, bf16[768,2304]{1,0:T(8,128)(2,1)} %wqkv.3, f32[1,2304]{1,0:T(1,128)} %fusion.1.bqkv, bf16[768,768]{1,0:T(8,128)(2,1)} %wout.3, ...), custom_call_target="tpu_custom_call" | custom-call | tf_op jit(solution)/shard_map/first/pallas_call | solution.py:364
  76.4 61.2 %middle.1 = (bf16[1024,768]{1,0:T(8,128)(2,1)}, f32[1024,768]{1,0:T(8,128)}, bf16[1024,768]{1,0:T(8,128)(2,1)}, bf16[768,3072]{1,0:T(8,128)(2,1)}, bf16[768,3072...) custom-call(f32[1024,768]{1,0:T(8,128)} %get-tuple-element.30.r1, ...), custom_call_target="tpu_custom_call" | custom-call | tf_op jit(solution)/shard_map/middle/pallas_call | solution.py:377
  137.6 2.4 copy.45
  140.1 36.1 %last.1 = (bf16[1024,768]{1,0:T(8,128)(2,1)}, bf16[768,2304]{1,0:T(8,128)(2,1)}, f32[8,768]{1,0:T(8,128)}) custom-call(bf16[1024,768]{1,0:T(8,128)(2,1)} %bitcast.29, s32[2,4]{1,0:T(2,128)} %copy.47.lens, bf16[1024,2304]{1,0:T(8,128)(2,1)} %get-tuple-element.33.qkv, bf16[1024,768]{1,0:T(8,128)(2,1)} %get-tuple-element.31.ctx, ...), custom_call_target="tpu_custom_call" | custom-call | tf_op jit(solution)/shard_map/last/pallas_call | solution.py:393
  176.2 5.8 copy.43
  185.5 38.2 %reduce-scatter.25.cloned.1.call-done = bf16[576,768]{1,0:T(8,128)(2,1)} async-done(((bf16[2304,768]{1,0:T(8,128)(2,1)}), bf16[576,768]{1,0:T(8,128)(2,1)}) %reduce-scatter.25.cloned.1.call-update) | async-done | bytes 884752
  223.7 1.5 copy.44
  225.2 1.4 convert_element_type.45
  226.7 47.4 %reduce-scatter.21.cloned.1.call-done = bf16[192,3072]{1,0:T(8,128)(2,1)} async-done(((bf16[768,3072]{1,0:T(8,128)(2,1)}), bf16[192,3072]{1,0:T(8,128)(2,1)}) %reduce-scatter.21.cloned.1.call-update) | async-done | bytes 1179664 | tf_op jit(solution)/shard_map/reduce_scatter | solution.py:414
  274.1 3.0 convert_element_type.48
  277.2 47.4 %reduce-scatter.17.cloned.1.call-done = bf16[768,768]{1,0:T(8,128)(2,1)} async-done(((bf16[768,3072]{1,0:T(8,128)(2,1)}), bf16[768,768]{1,0:T(8,128)(2,1)}) %reduce-scatter.17.cloned.1.call-update) | async-done | bytes 1179664 | tf_op jit(solution)/shard_map/reduce_scatter | solution.py:414
  324.6 2.9 convert_element_type.47
  327.5 1.4 copy-done.2
  328.8 2.8 copy.39
  331.6 3.7 all-to-all-start.2
  335.3 2.8 copy.41
  338.1 17.3 %all-to-all-done.2 = bf16[2,512,768]{2,0,1:T(2,128)(2,1)S(1)} async-done(((bf16[2,512,768]{2,0,1:T(2,128)(2,1)}), bf16[2,512,768]{2,0,1:T(2,128)(2,1)S(1)}, u32[]{:S(2)}, u32[]{:S(2)}) %all-to-all-start.2) | async-done | bytes 1572896 | tf_op jit(solution)/shard_map/all_to_all | solution.py:405
  355.4 3.6 all-to-all-start.3
  359.0 55.4 %all-reduce = (f32[8,768]{1,0:T(8,128)S(1)}, f32[8,768]{1,0:T(8,128)S(1)}, f32[1,3072]{1,0:T(1,128)S(1)}) all-reduce(f32[8,768]{1,0:T(8,128)S(1)} %copy-done.5, f32[8,768]{1,0:T(8,128)S(1)} %copy-done.4, f32[1,3072]{1,0:T(1,128)S(1)} %copy-done.6), channel_id=1, replica_groups=mesh['rows'=8,'heads'=4] {'rows','heads'}, use_global_device_ids=true, to_apply=%region_2.0 | all-reduce | flops 15360 | bytes 122880 | tf_op jit(solution)/shard_map/psum | solution.py:410
  416.3 1.3 copy.40
  418.7 2.0 copy.42
  420.7 1.5 broadcast_multiply_fusion.2
  422.3 37.7 %reduce-scatter.13.cloned.1.call-done = f32[96,576]{1,0:T(8,128)} async-done(((f32[768,576]{1,0:T(8,128)}), f32[96,576]{1,0:T(8,128)}) %reduce-scatter.13.cloned.1.call-update) | async-done | bytes 221200 | tf_op jit(solution)/shard_map/reduce_scatter | solution.py:415
  460.0 1.7 broadcast_multiply_fusion.1
  461.6 69.7 %reduce-scatter.23.cloned.1.call-done = f32[192,384]{1,0:T(8,128)} async-done(((f32[192,3072]{1,0:T(8,128)}), f32[192,384]{1,0:T(8,128)}) %reduce-scatter.23.cloned.1.call-update) | async-done | bytes 294928 | tf_op jit(solution)/shard_map/reduce_scatter | solution.py:415
  531.3 1.7 multiply_bitcast_fusion
  533.0 69.8 %reduce-scatter.19.cloned.1.call-done = f32[96,768]{1,0:T(8,128)} async-done(((f32[768,768]{1,0:T(8,128)}), f32[96,768]{1,0:T(8,128)}) %reduce-scatter.19.cloned.1.call-update) | async-done | bytes 294928 | tf_op jit(solution)/shard_map/reduce_scatter | solution.py:415
  602.8 1.7 broadcast_multiply_fusion
  (74 shorter events, 11.2 us)
Async XLA Ops:
  7.2 28.2 %copy-start = (s32[8,4]{0,1:T(4,128)S(1)}, s32[8,4]{0,1:T(4,128)}, u32[]{:S(2)}) copy-start(s32[8,4]{0,1:T(4,128)} %param.17) | copy-start | bytes 388
  31.5 4.6 copy-start.8
  31.5 4.6 copy-start.9
  31.5 4.6 copy-start.10
  31.5 5.2 copy-start.11
  31.5 5.2 copy-start.12
  31.5 5.2 copy-start.13
  31.5 5.2 copy-start.14
  31.5 5.2 copy-start.15
  31.6 5.9 copy-start.7
  31.6 23.8 %all-to-all-start.1 = ((bf16[8,128,768]{2,1,0:T(8,128)(2,1)}), bf16[8,128,768]{2,1,0:T(8,128)(2,1)S(1)}, u32[]{:S(2)}, u32[]{:S(2)}) async-start(bf16[8,128,768]{2,1,0:T(8,128)(2,1)} %param.31), calls=%async_computation.1 | async-start | bytes 3145728 | tf_op jit(solution)/shard_map/all_to_all | solution.py:361
  35.3 148.1 %reduce-scatter.27.cloned.1.call-start = ((), (), s32[]{:S(2)}) async-start(), calls=%async_computation.19 | async-start | bytes 1474560
  140.0 83.7 %reduce-scatter.25.cloned.1.call-start = ((), (), s32[]{:S(2)}) async-start(), calls=%async_computation.18 | async-start | bytes 4423680
  182.0 92.1 %reduce-scatter.21.cloned.1.call-start = ((), (), s32[]{:S(2)}) async-start(), calls=%async_computation.16 | async-start | bytes 5898240 | tf_op jit(solution)/shard_map/reduce_scatter | solution.py:414
  182.7 141.8 %reduce-scatter.17.cloned.1.call-start = ((), (), s32[]{:S(2)}) async-start(), calls=%async_computation.14 | async-start | bytes 5898240 | tf_op jit(solution)/shard_map/reduce_scatter | solution.py:414
  183.3 237.4 %reduce-scatter.15.cloned.1.call-start = ((), (), s32[]{:S(2)}) async-start(), calls=%async_computation.13 | async-start | bytes 884736 | tf_op jit(solution)/shard_map/reduce_scatter | solution.py:415
  185.5 274.5 %reduce-scatter.13.cloned.1.call-start = ((), (), s32[]{:S(2)}) async-start(), calls=%async_computation.12 | async-start | bytes 2211840 | tf_op jit(solution)/shard_map/reduce_scatter | solution.py:415
  226.7 304.7 %reduce-scatter.23.cloned.1.call-start = ((), (), s32[]{:S(2)}) async-start(), calls=%async_computation.17 | async-start | bytes 2654208 | tf_op jit(solution)/shard_map/reduce_scatter | solution.py:415
  277.1 325.7 %reduce-scatter.19.cloned.1.call-start = ((), (), s32[]{:S(2)}) async-start(), calls=%async_computation.15 | async-start | bytes 2654208 | tf_op jit(solution)/shard_map/reduce_scatter | solution.py:415
  327.4 1.4 copy-start.2
  331.6 3.7 copy-start.3
  331.6 23.7 %all-to-all-start.2 = ((bf16[2,512,768]{2,0,1:T(2,128)(2,1)}), bf16[2,512,768]{2,0,1:T(2,128)(2,1)S(1)}, u32[]{:S(2)}, u32[]{:S(2)}) async-start(bf16[2,512,768]{2,0,1:T(2,128)(2,1)} %copy.39), calls=%async_computation.2 | async-start | bytes 3145728 | tf_op jit(solution)/shard_map/all_to_all | solution.py:405
  338.1 20.9 %copy-start.4 = (f32[8,768]{1,0:T(8,128)S(1)}, f32[8,768]{1,0:T(8,128)}, u32[]{:S(2)}) copy-start(f32[8,768]{1,0:T(8,128)} %get-tuple-element.41) | copy-start | bytes 73732
  338.1 20.9 %copy-start.5 = (f32[8,768]{1,0:T(8,128)S(1)}, f32[8,768]{1,0:T(8,128)}, u32[]{:S(2)}) copy-start(f32[8,768]{1,0:T(8,128)} %get-tuple-element.39) | copy-start | bytes 73732
  338.1 20.9 %copy-start.6 = (f32[1,3072]{1,0:T(1,128)S(1)}, f32[1,3072]{1,0:T(1,128)}, u32[]{:S(2)}) copy-start(f32[1,3072]{1,0:T(1,128)} %get-tuple-element.43) | copy-start | bytes 36868
  355.4 62.3 %all-to-all-start.3 = ((bf16[2,512,768]{2,0,1:T(2,128)(2,1)}), bf16[2,512,768]{2,0,1:T(2,128)(2,1)S(1)}, u32[]{:S(2)}, u32[]{:S(2)}) async-start(bf16[2,512,768]{2,0,1:T(2,128)(2,1)} %copy.41), calls=%async_computation.3 | async-start | bytes 3145728 | tf_op jit(solution)/shard_map/all_to_all | solution.py:405
  418.7 185.8 %copy-start.1 = (s32[8,4]{0,1:T(4,128)S(1)}, s32[8,4]{0,1:T(4,128)}, u32[]{:S(2)}) copy-start(s32[8,4]{0,1:T(4,128)} %param.17) | copy-start | bytes 388
Sparse Core Ops, SparseCore 0:
  140.2 26.7 reduce-scatter.26
  182.1 41.5 reduce-scatter.24
  226.2 47.8 reduce-scatter.20
  276.7 47.8 reduce-scatter.16
  327.7 62.5 reduce-scatter.14
  394.0 65.9 reduce-scatter.12
  463.5 67.8 reduce-scatter.22
  534.8 67.9 reduce-scatter.18
